TPU v7x, 32 devices: a whole 2x2x4 slice. The times are simulated.
32 devices in a mesh: groups: 2 (over y), seq: 4 (over z), dp: 4 (over x, core).
Axes of the slice: x: 2, y: 2, z: 4, core: 2. Of those that a mesh axis runs over, the one named last changes fastest.
Arguments:
- inputs: bfloat16 [8, 4096, 448], P(('groups', 'dp'), 'seq'), parts along dimension 0, may hold values from -6 to 6
- cotangent: bfloat16 [8, 4096, 448], P(('groups', 'dp'), 'seq'), parts along dimension 0, may hold values from -6 to 6
- first_weight_matrix: bfloat16 [3, 448, 448], P(None, None, 'dp'), may hold values from -0.15625 to 0.15625
- weight_two: bfloat16 [3, 448, 448], P(None, None, 'dp'), may hold values from -0.15625 to 0.15625
Outputs:
- input_grad: bfloat16 [8, 4096, 448], P(('groups', 'dp'), 'seq'), parts along dimension 0
- grad_one: float32 [6, 448, 448], P('groups', None, 'dp'), parts along dimension 0
- grad_two: float32 [6, 448, 448], P('groups', None, 'dp'), parts along dimension 0
There are 2 independent parts, one for each index of `groups`. A program takes and returns all parts, laid end to end along the dimension named above; an argument that names none is the same for every part. Nothing has to cross between parts.
All inputs are finite; a program needn't handle non-finite values.
Results may differ from a plain program's by a relative error of at most 0.012.
Values may be sent and summed in bfloat16 or wider, within the bound.
No kernel may reach another device: no remote copies, remote signals or barrier semaphores. Data moves between devices by JAX's collectives and lax.ppermute only.
A program may use at most 64 MiB of HBM per device.

v0:
```python
import math
import jax
import jax.numpy as jnp
from jax import lax
from jax.sharding import PartitionSpec as P


def shifted(block, axis, distance):
    devices = range(lax.axis_size(axis))
    route = [(i - distance, i) for i in devices if i - distance in devices]
    return lax.ppermute(block, axis, route)


def gelu_slope(value):
    return jax.vjp(jax.nn.gelu, value)[1](jnp.ones_like(value))[0]


def outer_terms(left, right, factor):
    product = lax.dot_general(
        left, right, (((0,), (0,)), ((), ())), preferred_element_type=jnp.float32
    )
    return product * factor


def back_product(tap, weight):
    return lax.dot_general(
        tap, weight, (((1,), (1,)), ((), ())), preferred_element_type=jnp.float32
    )


def on_device(inputs, cotangent, first_weight_matrix, weight_two):
    chans = inputs.shape[2]
    rows = inputs.shape[0] * inputs.shape[1]
    factor = 1.0 / math.sqrt(
        inputs.shape[0] * lax.axis_size("dp") * inputs.shape[1] * lax.axis_size("seq")
    )
    full_one = lax.all_gather(first_weight_matrix, "dp", axis=2, tiled=True)
    flat_in = inputs.reshape(rows, chans)
    inputs_f = flat_in.astype(jnp.float32)
    input_activation = jax.nn.gelu(inputs_f).astype(jnp.bfloat16)
    act_before = shifted(input_activation, "seq", 2)
    act_after = shifted(input_activation, "seq", -2)
    flat_cot = cotangent.reshape(rows, chans)
    cot_later = shifted(flat_cot, "seq", -4)
    cot_earlier = shifted(flat_cot, "seq", 4)
    preactivation = jnp.dot(act_before, full_one[0], preferred_element_type=jnp.float32)
    preactivation = preactivation + jnp.dot(
        input_activation, full_one[1], preferred_element_type=jnp.float32
    )
    preactivation = preactivation + jnp.dot(
        act_after, full_one[2], preferred_element_type=jnp.float32
    )
    hidden_f = (inputs_f + preactivation).astype(jnp.bfloat16).astype(jnp.float32)
    act_one = jax.nn.gelu(hidden_f).astype(jnp.bfloat16)
    full_two = lax.all_gather(weight_two, "dp", axis=2, tiled=True)
    second_layer_taps = (cot_later, flat_cot, cot_earlier)
    delta_one = back_product(second_layer_taps[0], full_two[0])
    delta_one = delta_one + back_product(second_layer_taps[1], full_two[1])
    delta_one = delta_one + back_product(second_layer_taps[2], full_two[2])
    middle_gradient = (flat_cot.astype(jnp.float32) + gelu_slope(hidden_f) * delta_one).astype(
        jnp.bfloat16
    )
    part_two = jnp.stack(
        [outer_terms(act_one, second_layer_taps[k], factor) for k in range(3)]
    ).astype(jnp.bfloat16)
    grad_two = lax.psum(
        lax.psum_scatter(part_two, "dp", scatter_dimension=2, tiled=True).astype(jnp.float32), "seq"
    )
    grad_later = shifted(middle_gradient, "seq", -2)
    grad_earlier = shifted(middle_gradient, "seq", 2)
    first_layer_taps = (grad_later, middle_gradient, grad_earlier)
    delta_zero = back_product(first_layer_taps[0], full_one[0])
    delta_zero = delta_zero + back_product(first_layer_taps[1], full_one[1])
    delta_zero = delta_zero + back_product(first_layer_taps[2], full_one[2])
    input_grad = (middle_gradient.astype(jnp.float32) + gelu_slope(inputs_f) * delta_zero).astype(
        jnp.bfloat16
    )
    part_one = jnp.stack(
        [outer_terms(input_activation, first_layer_taps[k], factor) for k in range(3)]
    ).astype(jnp.bfloat16)
    grad_one = lax.psum(
        lax.psum_scatter(part_one, "dp", scatter_dimension=2, tiled=True).astype(jnp.float32), "seq"
    )
    return (input_grad.reshape(inputs.shape), grad_one, grad_two)


def solution(mesh):
    placed = (
        P(("groups", "dp"), "seq", None),
        P(("groups", "dp"), "seq", None),
        P(None, None, "dp"),
        P(None, None, "dp"),
    )
    return jax.shard_map(
        on_device,
        mesh=mesh,
        in_specs=placed,
        out_specs=(
            P(("groups", "dp"), "seq", None),
            P("groups", None, "dp"),
            P("groups", None, "dp"),
        ),
        check_vma=False,
    )
```

profile of v0, /device:TPU:0, one launch (start us, length us, event | category | flops | bytes accessed | tf_op | source)
XLA Modules:
  0.0 242.5 jit_solution(234301999639612765)
XLA Ops:
  7.2 0.0 copy-start.2
  7.2 0.0 all-gather.3.cloned.1.call-start
  7.2 2.2 copy.9
  9.4 0.0 all-gather.3.cloned.1.call-update
  9.4 0.0 all-gather.5.cloned.1.call-start
  9.5 2.1 copy.13
  11.6 0.0 all-gather.5.cloned.1.call-update
  11.6 0.0 reduce-scatter.9.cloned.1.call-start
  11.7 1.6 fusion.26
  13.2 6.9 %collective-permute-start = (bf16[1024,448]{0,1:T(8,128)(2,1)}, bf16[1024,448]{0,1:T(8,128)(2,1)}, u32[]{:S(2)}, u32[]{:S(2)}) collective-permute-start(bf16[1024,448]{0,1:T(8,128)(2,1)} %fusion.26), channel_id=1, source_target_pairs={{0,8},{4,12},{1,9},{5,13},{2,10},{6,14},{3,11},{7,15},{16,24},{20,... | collective-permute-start | bytes 2752520 | tf_op jit(solution)/shard_map/ppermute | solution.py:11
  20.1 1.3 collective-permute-start.1
  21.4 1.6 collective-permute-start.2
  23.0 11.0 %all-gather.3.cloned.1.call-done = bf16[3,448,448]{1,0,2:T(4,128)(2,1)} async-done(((bf16[3,448,112]{1,0,2:T(4,128)(2,1)}), bf16[3,448,448]{1,0,2:T(4,128)(2,1)}) %all-gather.3.cloned.1.call-update) | async-done | bytes 1204240 | tf_op jit(solution)/shard_map/all_gather | solution.py:37
  34.0 6.1 %fusion.88 = (bf16[1,448,448]{1,0,2:T(2,128)(2,1)S(1)}, bf16[1,448,448]{1,0,2:T(2,128)(2,1)S(1)}, bf16[1,448,448]{1,0,2:T(2,128)(2,1)}) fusion(bf16[3,448,448]{1,0,2:T(4,128)(2,1)} %all-gather.3.cloned.1.call-done), kind=kLoop, calls=%fused_computation.93 | loop fusion | bytes 2408448 | tf_op jit(solution)/shard_map/slice | solution.py:51
  40.1 17.2 %all-gather.5.cloned.1.call-done = bf16[3,448,448]{1,0,2:T(4,128)(2,1)} async-done(((bf16[3,448,112]{1,0,2:T(4,128)(2,1)}), bf16[3,448,448]{1,0,2:T(4,128)(2,1)}) %all-gather.5.cloned.1.call-update) | async-done | bytes 1204240 | tf_op jit(solution)/shard_map/all_gather | solution.py:55
  57.3 6.3 %fusion.87 = (bf16[1,448,448]{1,0,2:T(2,128)(2,1)}, bf16[1,448,448]{1,0,2:T(2,128)(2,1)}, bf16[1,448,448]{1,0,2:T(2,128)(2,1)}) fusion(bf16[3,448,448]{1,0,2:T(4,128)(2,1)} %all-gather.5.cloned.1.call-done), kind=kLoop, calls=%fused_computation.92 | loop fusion | bytes 2408448 | tf_op jit(solution)/shard_map/slice | solution.py:59
  63.6 2.4 copy.21
  66.0 2.0 copy.22
  68.0 1.9 copy.23
  69.9 3.5 %copy.24 = bf16[1,448,448]{2,1,0:T(8,128)(2,1)} copy(bf16[1,448,448]{1,0,2:T(2,128)(2,1)} %get-tuple-element.7) | data formatting | bytes 802816
  73.4 1.3 copy.25
  74.7 1.0 fusion.46
  75.7 3.1 %fusion.57 = f32[1024,448]{0,1:T(8,128)} fusion(bf16[1,448,448]{2,1,0:T(8,128)(2,1)S(1)} %copy.25, bf16[1,1024,448]{1,2,0:T(8,128)(2,1)} %param.5), kind=kOutput, calls=%fused_computation.71 | convolution fusion | flops 411041792 | bytes 3153920 | tf_op jit(solution)/shard_map/dot_general | solution.py:26
  78.8 1.9 fusion.74
  80.8 2.1 fusion.27
  82.8 0.0 copy-start.17
  82.8 2.3 fusion.40
  85.2 2.0 fusion.41
  87.2 0.2 pad_maximum_fusion.1
  87.4 1.8 copy.19
  89.2 2.5 %reshape.22 = bf16[448,1344]{1,0:T(8,128)(2,1)} reshape(bf16[448,3,448]{2,1,0:T(4,128)(2,1)S(1)} %bitcast.119) | data formatting | bytes 2408448
  91.7 0.0 reduce-scatter.9.cloned.1.call-update
  91.8 0.2 reduce-scatter.7.cloned.1.call-start
  92.0 3.2 %fusion.59 = f32[1024,448]{0,1:T(8,128)} fusion(bf16[1024,448]{0,1:T(8,128)(2,1)} %collective-permute-done.2, bf16[1,448,448]{2,1,0:T(8,128)(2,1)S(1)} %copy-done.10), kind=kOutput, calls=%fused_computation.73 | convolution fusion | flops 411041792 | bytes 3153920 | tf_op jit(solution)/shard_map/dot_general | solution.py:26
  95.2 1.3 copy.26
  96.5 0.0 copy-start.3
  96.5 4.2 %fusion.17 = bf16[1024,448]{0,1:T(8,128)(2,1)S(1)} fusion(bf16[1024,448]{0,1:T(8,128)(2,1)} %copy-done.17, f32[1024,448]{0,1:T(8,128)} %fusion.59, f32[1024,448]{0,1:T(8,128)S(1)} %copy-done.7, bf16[1024,448]{0,1:T(8,128)(2,1)} %collective-permute-done.2, bf16[1,448,448]{2,1,0:T(8,128)(2,1)S(1)} %copy.26, bf16[1,1024,448]{1,2,0:T(8,128)(2,1)} %param.5), kind=kOutput, calls=%fused_computation.27 | convolution fusion | flops 422051840 | bytes 7741440 | tf_op jit(solution)/shard_map/dot_general | solution.py:26
  100.7 4.5 %collective-permute-start.4 = (bf16[1024,448]{0,1:T(8,128)(2,1)S(1)}, bf16[1024,448]{0,1:T(8,128)(2,1)S(1)}, u32[]{:S(2)}, u32[]{:S(2)}) collective-permute-start(bf16[1024,448]{0,1:T(8,128)(2,1)S(1)} %fusion.17), channel_id=1, source_target_pairs={{0,8},{4,12},{1,9},{5,13},{2,10},{6,14},{3,11},{7,15},{16,24},{20,... | collective-permute-start | bytes 2752520 | tf_op jit(solution)/shard_map/ppermute | solution.py:11
  105.2 1.3 collective-permute-start.3
  106.5 0.8 fusion.43
  107.4 17.8 %collective-permute-done.4 = bf16[1024,448]{0,1:T(8,128)(2,1)S(1)} collective-permute-done((bf16[1024,448]{0,1:T(8,128)(2,1)S(1)}, bf16[1024,448]{0,1:T(8,128)(2,1)S(1)}, u32[]{:S(2)}, u32[]{:S(2)}) %collective-permute-start.4) | collective-permute-done | bytes 917536 | tf_op jit(solution)/shard_map/ppermute | solution.py:11
  125.2 0.8 fusion.42
  126.0 0.1 copy-done.18
  126.1 23.8 %collective-permute-done.3 = bf16[1024,448]{0,1:T(8,128)(2,1)S(1)} collective-permute-done((bf16[1024,448]{0,1:T(8,128)(2,1)S(1)}, bf16[1024,448]{0,1:T(8,128)(2,1)S(1)}, u32[]{:S(2)}, u32[]{:S(2)}) %collective-permute-start.3) | collective-permute-done | bytes 917536 | tf_op jit(solution)/shard_map/ppermute | solution.py:11
  149.9 0.9 copy-done.15
  150.8 0.8 fusion.44
  151.6 0.2 pad_maximum_fusion
  151.8 1.8 copy.17
  153.6 2.5 %reshape.20 = bf16[448,1344]{1,0:T(8,128)(2,1)} reshape(bf16[448,3,448]{2,1,0:T(4,128)(2,1)S(1)} %bitcast.120) | data formatting | bytes 2408448
  156.1 0.0 reduce-scatter.7.cloned.1.call-update
  156.2 0.6 fusion.69
  156.9 0.4 copy-done.1
  157.2 0.3 copy-done.16
  157.5 0.6 fusion.72
  158.2 0.5 copy-done.4
  158.7 0.1 copy-done.12
  158.8 0.5 copy-done.19
  159.3 2.7 %fusion.52 = bf16[1,1024,448]{1,2,0:T(8,128)(2,1)} fusion(f32[1024,448]{0,1:T(8,128)S(1)} %fusion.72, f32[1024,448]{0,1:T(8,128)S(1)} %fusion.69, bf16[1,1024,448]{1,2,0:T(8,128)(2,1)S(1)} %copy-done.4, bf16[1024,448]{0,1:T(8,128)(2,1)S(1)} %copy-done.14, bf16[1024,448]{0,1:T(8,128)(2,1)S(1)} %copy-done.19, bf16[1,448,448]{2,1,0:T(8,128)(2,1)S(1)} %copy-done.12), kind=kOutput, calls=%fused_computation.68 | convolution fusion | flops 422051840 | bytes 7741440 | tf_op jit(solution)/shard_map/dot_general | solution.py:26
  162.0 1.7 reshape.23
  163.7 0.3 copy.20
  164.0 15.7 %reduce-scatter.7.cloned.1.call-done = bf16[112,1344]{1,0:T(8,128)(2,1)} async-done(((bf16[448,1344]{1,0:T(8,128)(2,1)}), bf16[112,1344]{1,0:T(8,128)(2,1)}) %reduce-scatter.7.cloned.1.call-update) | async-done | bytes 301072
  179.8 1.7 reshape.21
  181.5 0.3 copy.18
  181.8 54.2 %all-reduce.2 = (f32[3,448,112]{2,1,0:T(8,128)}, f32[3,448,112]{2,1,0:T(8,128)}) all-reduce(bf16[3,448,112]{2,1,0:T(8,128)(2,1)S(1)} %copy.18, bf16[3,448,112]{2,1,0:T(8,128)(2,1)S(1)} %copy.20), channel_id=1, replica_groups=mesh['groups'=2,'seq'=4,'dp'=4] {'seq'}, use_global_device_ids=true, to_apply=%region_1.0 | all-reduce | flops 301056 | bytes 1806336 | tf_op jit(solution)/shard_map/psum | solution.py:81
  (34 shorter events, 0.1 us)
Async XLA Ops:
  7.2 4.5 %copy-start.2 = (bf16[1,1024,448]{1,2,0:T(8,128)(2,1)S(1)}, bf16[1,1024,448]{1,2,0:T(8,128)(2,1)}, u32[]{:S(2)}) copy-start(bf16[1,1024,448]{1,2,0:T(8,128)(2,1)} %param.4) | copy-start | bytes 2752516
  7.2 26.8 %all-gather.3.cloned.1.call-start = ((), (), s32[]{:S(2)}) async-start(), calls=%async_computation.2 | async-start | bytes 2293760 | tf_op jit(solution)/shard_map/all_gather | solution.py:37
  9.4 47.9 %all-gather.5.cloned.1.call-start = ((), (), s32[]{:S(2)}) async-start(), calls=%async_computation.3 | async-start | bytes 2293760 | tf_op jit(solution)/shard_map/all_gather | solution.py:55
  11.6 150.4 %reduce-scatter.9.cloned.1.call-start = ((), (), s32[]{:S(2)}) async-start(), calls=%async_computation.5 | async-start | bytes 1576960
  13.2 65.6 %collective-permute-start = (bf16[1024,448]{0,1:T(8,128)(2,1)}, bf16[1024,448]{0,1:T(8,128)(2,1)}, u32[]{:S(2)}, u32[]{:S(2)}) collective-permute-start(bf16[1024,448]{0,1:T(8,128)(2,1)} %fusion.26), channel_id=1, source_target_pairs={{0,8},{4,12},{1,9},{5,13},{2,10},{6,14},{3,11},{7,15},{16,24},{20,... | collective-permute-start | bytes 2752520 | tf_op jit(solution)/shard_map/ppermute | solution.py:11
  20.1 60.7 %collective-permute-start.1 = (bf16[1024,448]{0,1:T(8,128)(2,1)}, bf16[1024,448]{0,1:T(8,128)(2,1)}, u32[]{:S(2)}, u32[]{:S(2)}) collective-permute-start(bf16[1024,448]{0,1:T(8,128)(2,1)} %fusion.26), channel_id=1, source_target_pairs={{8,0},{12,4},{9,1},{13,5},{10,2},{14,6},{11,3},{15,7},{24,16},{28,... | collective-permute-start | bytes 2752520 | tf_op jit(solution)/shard_map/ppermute | solution.py:11
  21.4 63.8 %collective-permute-start.2 = (bf16[1024,448]{0,1:T(8,128)(2,1)}, bf16[1024,448]{0,1:T(8,128)(2,1)}, u32[]{:S(2)}, u32[]{:S(2)}) collective-permute-start(bf16[1024,448]{0,1:T(8,128)(2,1)} %bitcast), channel_id=1, source_target_pairs={} | collective-permute-start | bytes 2752520 | tf_op jit(solution)/shard_map/ppermute | solution.py:11
  66.0 12.8 %copy-start = (bf16[1,448,448]{2,1,0:T(8,128)(2,1)}, bf16[1,448,448]{2,1,0:T(8,128)(2,1)S(1)}, u32[]{:S(2)}) copy-start(bf16[1,448,448]{2,1,0:T(8,128)(2,1)S(1)} %copy.21) | copy-start | bytes 1204228
  68.0 5.4 %copy-start.6 = (bf16[1,448,448]{1,0,2:T(2,128)(2,1)S(1)}, bf16[1,448,448]{1,0,2:T(2,128)(2,1)}, u32[]{:S(2)}) copy-start(bf16[1,448,448]{1,0,2:T(2,128)(2,1)} %get-tuple-element.6) | copy-start | bytes 1204228
  69.9 4.8 %copy-start.8 = (bf16[1,448,448]{2,1,0:T(8,128)(2,1)S(1)}, bf16[1,448,448]{2,1,0:T(8,128)(2,1)}, u32[]{:S(2)}) copy-start(bf16[1,448,448]{2,1,0:T(8,128)(2,1)} %copy.22) | copy-start | bytes 1204228
  78.8 1.9 copy-start.11
  82.8 2.4 copy-start.17
  89.2 2.8 %copy-start.10 = (bf16[1,448,448]{2,1,0:T(8,128)(2,1)S(1)}, bf16[1,448,448]{2,1,0:T(8,128)(2,1)}, u32[]{:S(2)}) copy-start(bf16[1,448,448]{2,1,0:T(8,128)(2,1)} %copy.24) | copy-start | bytes 1204228
  91.7 3.4 %copy-start.5 = (bf16[1,448,448]{1,0,2:T(2,128)(2,1)S(1)}, bf16[1,448,448]{1,0,2:T(2,128)(2,1)}, u32[]{:S(2)}) copy-start(bf16[1,448,448]{1,0,2:T(2,128)(2,1)} %get-tuple-element.5) | copy-start | bytes 1204228
  91.7 4.8 %copy-start.7 = (f32[1024,448]{0,1:T(8,128)S(1)}, f32[1024,448]{0,1:T(8,128)}, u32[]{:S(2)}) copy-start(f32[1024,448]{0,1:T(8,128)} %fusion.57) | copy-start | bytes 5505028
  91.8 88.0 %reduce-scatter.7.cloned.1.call-start = ((), (), s32[]{:S(2)}) async-start(), calls=%async_computation.4 | async-start | bytes 1576960
  96.5 10.0 %copy-start.3 = (bf16[1,1024,448]{1,2,0:T(8,128)(2,1)S(1)}, bf16[1,1024,448]{1,2,0:T(8,128)(2,1)}, u32[]{:S(2)}) copy-start(bf16[1,1024,448]{1,2,0:T(8,128)(2,1)} %param.4) | copy-start | bytes 2752516
  100.7 6.7 %copy-start.13 = (bf16[1024,448]{0,1:T(8,128)(2,1)}, bf16[1024,448]{0,1:T(8,128)(2,1)S(1)}, u32[]{:S(2)}) copy-start(bf16[1024,448]{0,1:T(8,128)(2,1)S(1)} %fusion.17) | copy-start | bytes 2752516
  100.7 24.5 %collective-permute-start.4 = (bf16[1024,448]{0,1:T(8,128)(2,1)S(1)}, bf16[1024,448]{0,1:T(8,128)(2,1)S(1)}, u32[]{:S(2)}, u32[]{:S(2)}) collective-permute-start(bf16[1024,448]{0,1:T(8,128)(2,1)S(1)} %fusion.17), channel_id=1, source_target_pairs={{0,8},{4,12},{1,9},{5,13},{2,10},{6,14},{3,11},{7,15},{16,24},{20,... | collective-permute-start | bytes 2752520 | tf_op jit(solution)/shard_map/ppermute | solution.py:11
  105.2 44.7 %collective-permute-start.3 = (bf16[1024,448]{0,1:T(8,128)(2,1)S(1)}, bf16[1024,448]{0,1:T(8,128)(2,1)S(1)}, u32[]{:S(2)}, u32[]{:S(2)}) collective-permute-start(bf16[1024,448]{0,1:T(8,128)(2,1)S(1)} %fusion.17), channel_id=1, source_target_pairs={{8,0},{12,4},{9,1},{13,5},{10,2},{14,6},{11,3},{15,7},{24,16},{28,... | collective-permute-start | bytes 2752520 | tf_op jit(solution)/shard_map/ppermute | solution.py:11
  125.2 0.9 copy-start.18
  149.9 0.9 copy-start.15
  153.6 2.5 %copy-start.9 = (bf16[1,448,448]{2,1,0:T(8,128)(2,1)S(1)}, bf16[1,448,448]{2,1,0:T(8,128)(2,1)}, u32[]{:S(2)}) copy-start(bf16[1,448,448]{2,1,0:T(8,128)(2,1)} %copy.22) | copy-start | bytes 1204228
  153.6 2.5 %copy-start.14 = (bf16[1024,448]{0,1:T(8,128)(2,1)S(1)}, bf16[1024,448]{0,1:T(8,128)(2,1)}, u32[]{:S(2)}) copy-start(bf16[1024,448]{0,1:T(8,128)(2,1)} %copy-done.13) | copy-start | bytes 2752516
  156.2 1.0 copy-start.1
  156.2 1.3 copy-start.16
  157.5 1.2 copy-start.4
  157.5 1.3 copy-start.12
  157.5 1.8 copy-start.19
Sparse Core Ops, SparseCore 0:
  10.1 23.8 all-gather.2
  36.1 21.1 all-gather.4
  91.9 26.2 reduce-scatter.8
  156.3 23.4 reduce-scatter.6
where the time goes:
time: 243 us
  waiting for transfers between devices  85.6 us (35%)
  blocking collectives  54.2 us (22%)
  local copies, waits for them, and re-layouts  44.6 us (18%)
  matrix products  26.1 us (11%)
  starting transfers between devices  15.9 us (7%)
  between operations  14.1 us (6%)
    psum x1, blocking collectives, on_device(): lax.psum(lax.psum_scatter(part_one, 'dp', scatter_dimension=2, tiled=True...  54.2 us
    ppermute x5, waiting for transfers between devices, shifted(): return lax.ppermute(block, axis, route)  41.6 us
    unnamed x56, local copies, waits for them, and re-layouts  32.2 us
    all_gather x1, waiting for transfers between devices, on_device(): full_two = lax.all_gather(weight_two, 'dp', axis=2, tiled=True)  17.2 us
    unnamed x6, waiting for transfers between devices  15.8 us
    ppermute x5, starting transfers between devices, shifted(): return lax.ppermute(block, axis, route)  15.6 us
    dot_general x6, matrix products, back_product(): lax.dot_general(tap, weight, (((1,), (1,)), ((), ())), preferred_element_...  14.4 us
    all_gather x1, waiting for transfers between devices, on_device(): full_one = lax.all_gather(first_weight_matrix, 'dp', axis=2, tiled=True)  11 us
  transfers between devices with their start and end apart: 9, of which 5 were waited for; matrix products, arithmetic and copies ran while one was open for 24% of the time, Pallas kernels for 0%

commit v1 on v0

--- a/solution.py
+++ b/solution.py
@@ -52,7 +52,14 @@
     )
     hidden_f = (inputs_f + preactivation).astype(jnp.bfloat16).astype(jnp.float32)
     act_one = jax.nn.gelu(hidden_f).astype(jnp.bfloat16)
-    full_two = lax.all_gather(weight_two, "dp", axis=2, tiled=True)
+    ways, here = (lax.axis_size("dp"), lax.axis_index("dp"))
+    full_two, reach = (weight_two, 1)
+    while reach < ways:
+        theirs = lax.ppermute(full_two, "dp", [(d, d ^ reach) for d in range(ways)])
+        mine_first = jnp.concatenate([full_two, theirs], axis=2)
+        theirs_first = jnp.concatenate([theirs, full_two], axis=2)
+        full_two = jnp.where(here & reach == 0, mine_first, theirs_first)
+        reach = 2 * reach
     second_layer_taps = (cot_later, flat_cot, cot_earlier)
     delta_one = back_product(second_layer_taps[0], full_two[0])
     delta_one = delta_one + back_product(second_layer_taps[1], full_two[1])

time: 243 us -> 222 us (0.914)
  local copies, waits for them, and re-layouts: 44.6 us -> 29.7 us
  waiting for transfers between devices: 85.6 us -> 78.4 us
  other arithmetic: 1.96 us -> 4.7 us
    all_gather x1 -> x0, waiting for transfers between devices: 17.2 us -> none  [on_device(): full_two = lax.all_gather(weight_two, 'dp', axis=2, tiled=True)]
    ppermute x0 -> x2, waiting for transfers between devices: none -> 16.8 us  [on_device(): theirs = lax.ppermute(full_two, 'dp', [(d, d ^ reach) for d in range(ways)])]
    all_gather x1, waiting for transfers between devices: 11 us -> 0.01 us  [on_device(): full_one = lax.all_gather(first_weight_matrix, 'dp', axis=2, tiled=True)]
    unnamed x56 -> x50, local copies, waits for them, and re-layouts: 32.2 us -> 23.6 us
    slice x1 -> x0, local copies, waits for them, and re-layouts: 6.33 us -> none  [on_device(): delta_one = delta_one + back_product(second_layer_taps[2], full_two[2])]
    ppermute x5, starting transfers between devices: 15.6 us -> 11.1 us  [shifted(): return lax.ppermute(block, axis, route)]
    ppermute x5, waiting for transfers between devices: 41.6 us -> 45.7 us  [shifted(): return lax.ppermute(block, axis, route)]
    ppermute x0 -> x2, starting transfers between devices: none -> 3.44 us  [on_device(): theirs = lax.ppermute(full_two, 'dp', [(d, d ^ reach) for d in range(ways)])]
  transfers between devices with their start and end apart: 9 -> 10, of which waited for: 5 -> 6; matrix products, arithmetic and copies ran while one was open for 24% -> 21% of each run, Pallas kernels for 0% -> 0%
where the time goes in v1:
time: 222 us; the launch traced here: 221 us
  waiting for transfers between devices  78.4 us (35%)
  blocking collectives  54.2 us (24%)
  local copies, waits for them, and re-layouts  29.7 us (13%)
  matrix products  25.2 us (11%)
  starting transfers between devices  14.9 us (7%)
  between operations  14.1 us (6%)
  other arithmetic  4.7 us (2%)
    psum x1, blocking collectives, on_device(): lax.psum(lax.psum_scatter(part_one, 'dp', scatter_dimension=2, tiled=True...  54.2 us
    ppermute x5, waiting for transfers between devices, shifted(): return lax.ppermute(block, axis, route)  45.7 us
    unnamed x50, local copies, waits for them, and re-layouts  23.6 us
    ppermute x2, waiting for transfers between devices, on_device(): theirs = lax.ppermute(full_two, 'dp', [(d, d ^ reach) for d in range(ways)])  16.8 us
    unnamed x5, waiting for transfers between devices  15.9 us
    dot_general x6, matrix products, back_product(): lax.dot_general(tap, weight, (((1,), (1,)), ((), ())), preferred_element_...  12.3 us
    ppermute x5, starting transfers between devices, shifted(): return lax.ppermute(block, axis, route)  11.1 us
    dot_general x5, matrix products, outer_terms(): lax.dot_general(left, right, (((0,), (0,)), ((), ())), preferred_element_...  6.8 us
  transfers between devices with their start and end apart: 10, of which 6 were waited for; matrix products, arithmetic and copies ran while one was open for 21% of the time, Pallas kernels for 0%

profile of v1, /device:TPU:0, one launch (start us, length us, event | category | flops | bytes accessed | tf_op | source)
XLA Modules:
  0.0 221.1 jit_solution(16981940895626397216)
XLA Ops:
  7.2 0.0 copy-start.4
  7.2 0.0 all-gather.2.cloned.1.call-start
  7.2 2.2 copy.8
  9.4 0.0 all-gather.2.cloned.1.call-update
  9.4 0.0 reduce-scatter.9.cloned.1.call-start
  9.5 0.5 collective-permute-start.2
  10.0 1.5 collective-permute-done.2
  11.5 1.7 maximum_select_fusion.1
  13.2 2.9 %collective-permute-start.3 = (bf16[3,448,224]{2,1,0:T(8,128)(2,1)S(1)}, bf16[3,448,224]{2,1,0:T(8,128)(2,1)S(1)}, u32[]{:S(2)}, u32[]{:S(2)}) collective-permute-start(bf16[3,448,224]{2,1,0:T(8,128)(2,1)S(1)} %maximum_select_fusion.1), channel_id=1, source_target_pairs={{0,2},{1,3},{2,0},{3,1},{4,6},{5,7},{6,4},{7,5},{8,10},{9,11},{10,... | collective-permute-start | bytes 1806344 | tf_op jit(solution)/shard_map/ppermute | solution.py:58
  16.1 1.6 fusion.26
  17.6 5.4 %collective-permute-start = (bf16[1024,448]{0,1:T(8,128)(2,1)}, bf16[1024,448]{0,1:T(8,128)(2,1)}, u32[]{:S(2)}, u32[]{:S(2)}) collective-permute-start(bf16[1024,448]{0,1:T(8,128)(2,1)} %fusion.26), channel_id=1, source_target_pairs={{0,8},{4,12},{1,9},{5,13},{2,10},{6,14},{3,11},{7,15},{16,24},{20,... | collective-permute-start | bytes 2752520 | tf_op jit(solution)/shard_map/ppermute | solution.py:11
  23.1 1.3 collective-permute-start.1
  24.4 1.6 collective-permute-start.4
  26.0 15.3 %collective-permute-done.3 = bf16[3,448,224]{2,1,0:T(8,128)(2,1)S(1)} collective-permute-done((bf16[3,448,224]{2,1,0:T(8,128)(2,1)S(1)}, bf16[3,448,224]{2,1,0:T(8,128)(2,1)S(1)}, u32[]{:S(2)}, u32[]{:S(2)}) %collective-permute-start.3) | collective-permute-done | bytes 602144 | tf_op jit(solution)/shard_map/ppermute | solution.py:58
  41.3 1.1 maximum_select_fusion
  42.4 1.1 copy-done.2
  43.5 3.1 %fusion.54 = f32[448,1024]{1,0:T(8,128)} fusion(bf16[3,448,448]{2,1,0:T(8,128)(2,1)S(1)} %maximum_select_fusion, bf16[1,1024,448]{1,2,0:T(8,128)(2,1)} %param.5), kind=kOutput, calls=%fused_computation.74 | convolution fusion | flops 411041792 | bytes 3211264 | tf_op jit(solution)/shard_map/dot_general | solution.py:26
  46.6 6.1 %fusion.82 = (bf16[1,448,448]{1,0,2:T(2,128)(2,1)S(1)}, bf16[1,448,448]{1,0,2:T(2,128)(2,1)S(1)}, bf16[1,448,448]{1,0,2:T(2,128)(2,1)}) fusion(bf16[3,448,448]{1,0,2:T(4,128)(2,1)} %all-gather.2.cloned.1.call-done), kind=kLoop, calls=%fused_computation.94 | loop fusion | bytes 2408448 | tf_op jit(solution)/shard_map/slice | solution.py:51
  52.6 2.4 %copy.16 = bf16[1,448,448]{2,1,0:T(8,128)(2,1)S(1)} copy(bf16[1,448,448]{1,0,2:T(2,128)(2,1)} %get-tuple-element.7) | data formatting | bytes 802816
  55.0 2.0 copy.17
  57.0 1.3 copy.18
  58.3 2.2 fusion.46
  60.5 1.9 fusion.69
  62.4 5.3 %collective-permute-done.1 = bf16[1024,448]{0,1:T(8,128)(2,1)} collective-permute-done((bf16[1024,448]{0,1:T(8,128)(2,1)}, bf16[1024,448]{0,1:T(8,128)(2,1)}, u32[]{:S(2)}, u32[]{:S(2)}) %collective-permute-start.1) | collective-permute-done | bytes 917536 | tf_op jit(solution)/shard_map/ppermute | solution.py:11
  67.7 2.1 fusion.27
  69.7 0.0 copy-start.15
  69.7 2.3 %fusion.40 = bf16[1,448,448]{2,1,0:T(8,128)(2,1)S(1)} fusion(bf16[1,1024,448]{1,2,0:T(8,128)(2,1)} %param.5, bf16[1024,448]{0,1:T(8,128)(2,1)S(1)} %fusion.27), kind=kOutput, calls=%fused_computation.58 | convolution fusion | flops 416030720 | bytes 2236416 | tf_op jit(solution)/shard_map/dot_general | solution.py:19
  72.1 2.0 fusion.41
  74.1 0.2 pad_maximum_fusion.1
  74.3 1.8 copy.14
  76.1 2.5 %reshape.22 = bf16[448,1344]{1,0:T(8,128)(2,1)} reshape(bf16[448,3,448]{2,1,0:T(4,128)(2,1)S(1)} %bitcast.121) | data formatting | bytes 2408448
  78.6 0.0 reduce-scatter.9.cloned.1.call-update
  78.6 0.2 reduce-scatter.7.cloned.1.call-start
  78.9 2.0 fusion.55
  80.9 0.0 copy-start.5
  80.9 3.3 %fusion.17 = bf16[1024,448]{0,1:T(8,128)(2,1)S(1)} fusion(bf16[1024,448]{0,1:T(8,128)(2,1)S(1)} %copy-done.16, f32[448,1024]{1,0:T(8,128)S(1)} %fusion.55, f32[448,1024]{1,0:T(8,128)S(1)} %copy-done.7, bf16[1024,448]{0,1:T(8,128)(2,1)} %collective-permute-done.4, bf16[3,448,448]{2,1,0:T(8,128)(2,1)S(1)} %copy-done.3, bf16[1,1024,448]{1,2,0:T(8,128)(2,1)} %param.5), kind=kOutput, calls=%fused_computation.27 | convolution fusion | flops 422051840 | bytes 7798784 | tf_op jit(solution)/shard_map/dot_general | solution.py:26
  84.2 1.5 collective-permute-start.6
  85.7 1.3 collective-permute-start.5
  87.0 0.8 fusion.43
  87.8 16.7 %collective-permute-done.6 = bf16[1024,448]{0,1:T(8,128)(2,1)S(1)} collective-permute-done((bf16[1024,448]{0,1:T(8,128)(2,1)S(1)}, bf16[1024,448]{0,1:T(8,128)(2,1)S(1)}, u32[]{:S(2)}, u32[]{:S(2)}) %collective-permute-start.6) | collective-permute-done | bytes 917536 | tf_op jit(solution)/shard_map/ppermute | solution.py:11
  104.5 0.8 fusion.42
  105.3 0.1 copy-done.17
  105.5 23.7 %collective-permute-done.5 = bf16[1024,448]{0,1:T(8,128)(2,1)S(1)} collective-permute-done((bf16[1024,448]{0,1:T(8,128)(2,1)S(1)}, bf16[1024,448]{0,1:T(8,128)(2,1)S(1)}, u32[]{:S(2)}, u32[]{:S(2)}) %collective-permute-start.5) | collective-permute-done | bytes 917536 | tf_op jit(solution)/shard_map/ppermute | solution.py:11
  129.2 0.8 fusion.44
  130.0 0.1 copy-done.13
  130.1 0.2 pad_maximum_fusion
  130.3 1.8 copy.12
  132.1 0.0 copy-start.8
  132.1 2.5 %reshape.20 = bf16[448,1344]{1,0:T(8,128)(2,1)} reshape(bf16[448,3,448]{2,1,0:T(4,128)(2,1)S(1)} %bitcast.122) | data formatting | bytes 2408448
  134.6 0.0 reduce-scatter.7.cloned.1.call-update
  134.7 0.6 fusion.64
  135.3 0.4 copy-done.1
  135.7 0.3 copy-done.14
  136.0 0.6 fusion.67
  136.6 0.5 copy-done.6
  137.2 0.1 copy-done.10
  137.3 0.4 copy-done.18
  137.7 2.7 %fusion.52 = bf16[1,1024,448]{1,2,0:T(8,128)(2,1)} fusion(f32[1024,448]{0,1:T(8,128)S(1)} %fusion.67, f32[1024,448]{0,1:T(8,128)S(1)} %fusion.64, bf16[1,1024,448]{1,2,0:T(8,128)(2,1)S(1)} %copy-done.6, bf16[1024,448]{0,1:T(8,128)(2,1)S(1)} %copy-done.12, bf16[1024,448]{0,1:T(8,128)(2,1)S(1)} %copy-done.18, bf16[1,448,448]{2,1,0:T(8,128)(2,1)S(1)} %copy-done.10), kind=kOutput, calls=%fused_computation.69 | convolution fusion | flops 422051840 | bytes 7741440 | tf_op jit(solution)/shard_map/dot_general | solution.py:26
  140.4 1.7 reshape.23
  142.2 0.3 copy.15
  142.5 15.8 %reduce-scatter.7.cloned.1.call-done = bf16[112,1344]{1,0:T(8,128)(2,1)} async-done(((bf16[448,1344]{1,0:T(8,128)(2,1)}), bf16[112,1344]{1,0:T(8,128)(2,1)}) %reduce-scatter.7.cloned.1.call-update) | async-done | bytes 301072
  158.3 1.7 reshape.21
  160.0 0.3 copy.13
  160.4 54.2 %all-reduce.2 = (f32[3,448,112]{2,1,0:T(8,128)}, f32[3,448,112]{2,1,0:T(8,128)}) all-reduce(bf16[3,448,112]{2,1,0:T(8,128)(2,1)S(1)} %copy.13, bf16[3,448,112]{2,1,0:T(8,128)(2,1)S(1)} %copy.15), channel_id=1, replica_groups=mesh['groups'=2,'seq'=4,'dp'=4] {'seq'}, use_global_device_ids=true, to_apply=%region_1.2 | all-reduce | flops 301056 | bytes 1806336 | tf_op jit(solution)/shard_map/psum | solution.py:88
  (30 shorter events, 0.1 us)
Async XLA Ops:
  7.2 8.9 %copy-start.4 = (bf16[1,1024,448]{1,2,0:T(8,128)(2,1)S(1)}, bf16[1,1024,448]{1,2,0:T(8,128)(2,1)}, u32[]{:S(2)}) copy-start(bf16[1,1024,448]{1,2,0:T(8,128)(2,1)} %param.4) | copy-start | bytes 2752516
  7.2 39.4 %all-gather.2.cloned.1.call-start = ((), (), s32[]{:S(2)}) async-start(), calls=%async_computation.2 | async-start | bytes 2293760 | tf_op jit(solution)/shard_map/all_gather | solution.py:37
  9.4 131.0 %reduce-scatter.9.cloned.1.call-start = ((), (), s32[]{:S(2)}) async-start(), calls=%async_computation.4 | async-start | bytes 1576960
  9.5 2.0 collective-permute-start.2
  13.2 28.2 %collective-permute-start.3 = (bf16[3,448,224]{2,1,0:T(8,128)(2,1)S(1)}, bf16[3,448,224]{2,1,0:T(8,128)(2,1)S(1)}, u32[]{:S(2)}, u32[]{:S(2)}) collective-permute-start(bf16[3,448,224]{2,1,0:T(8,128)(2,1)S(1)} %maximum_select_fusion.1), channel_id=1, source_target_pairs={{0,2},{1,3},{2,0},{3,1},{4,6},{5,7},{6,4},{7,5},{8,10},{9,11},{10,... | collective-permute-start | bytes 1806344 | tf_op jit(solution)/shard_map/ppermute | solution.py:58
  17.6 42.9 %collective-permute-start = (bf16[1024,448]{0,1:T(8,128)(2,1)}, bf16[1024,448]{0,1:T(8,128)(2,1)}, u32[]{:S(2)}, u32[]{:S(2)}) collective-permute-start(bf16[1024,448]{0,1:T(8,128)(2,1)} %fusion.26), channel_id=1, source_target_pairs={{0,8},{4,12},{1,9},{5,13},{2,10},{6,14},{3,11},{7,15},{16,24},{20,... | collective-permute-start | bytes 2752520 | tf_op jit(solution)/shard_map/ppermute | solution.py:11
  23.1 44.6 %collective-permute-start.1 = (bf16[1024,448]{0,1:T(8,128)(2,1)}, bf16[1024,448]{0,1:T(8,128)(2,1)}, u32[]{:S(2)}, u32[]{:S(2)}) collective-permute-start(bf16[1024,448]{0,1:T(8,128)(2,1)} %fusion.26), channel_id=1, source_target_pairs={{8,0},{12,4},{9,1},{13,5},{10,2},{14,6},{11,3},{15,7},{24,16},{28,... | collective-permute-start | bytes 2752520 | tf_op jit(solution)/shard_map/ppermute | solution.py:11
  24.4 47.7 %collective-permute-start.4 = (bf16[1024,448]{0,1:T(8,128)(2,1)}, bf16[1024,448]{0,1:T(8,128)(2,1)}, u32[]{:S(2)}, u32[]{:S(2)}) collective-permute-start(bf16[1024,448]{0,1:T(8,128)(2,1)} %bitcast), channel_id=1, source_target_pairs={} | collective-permute-start | bytes 2752520 | tf_op jit(solution)/shard_map/ppermute | solution.py:11
  42.4 1.1 copy-start.2
  55.0 5.5 %copy-start = (bf16[1,448,448]{2,1,0:T(8,128)(2,1)}, bf16[1,448,448]{2,1,0:T(8,128)(2,1)S(1)}, u32[]{:S(2)}) copy-start(bf16[1,448,448]{2,1,0:T(8,128)(2,1)S(1)} %copy.16) | copy-start | bytes 1204228
  58.3 9.4 %copy-start.9 = (bf16[1,448,448]{2,1,0:T(8,128)(2,1)}, bf16[1,448,448]{2,1,0:T(8,128)(2,1)S(1)}, u32[]{:S(2)}) copy-start(bf16[1,448,448]{2,1,0:T(8,128)(2,1)S(1)} %copy.18) | copy-start | bytes 1204228
  69.7 2.4 %copy-start.15 = (bf16[1024,448]{0,1:T(8,128)(2,1)}, bf16[1024,448]{0,1:T(8,128)(2,1)S(1)}, u32[]{:S(2)}) copy-start(bf16[1024,448]{0,1:T(8,128)(2,1)S(1)} %fusion.27) | copy-start | bytes 2752516
  76.1 2.8 %copy-start.3 = (bf16[3,448,448]{2,1,0:T(8,128)(2,1)S(1)}, bf16[3,448,448]{2,1,0:T(8,128)(2,1)}, u32[]{:S(2)}) copy-start(bf16[3,448,448]{2,1,0:T(8,128)(2,1)} %copy-done.2) | copy-start | bytes 3612676
  78.6 2.2 %copy-start.7 = (f32[448,1024]{1,0:T(8,128)S(1)}, f32[448,1024]{1,0:T(8,128)}, u32[]{:S(2)}) copy-start(f32[448,1024]{1,0:T(8,128)} %fusion.54) | copy-start | bytes 5505028
  78.6 79.7 %reduce-scatter.7.cloned.1.call-start = ((), (), s32[]{:S(2)}) async-start(), calls=%async_computation.3 | async-start | bytes 1576960
  78.9 2.0 copy-start.16
  80.9 6.1 %copy-start.5 = (bf16[1,1024,448]{1,2,0:T(8,128)(2,1)S(1)}, bf16[1,1024,448]{1,2,0:T(8,128)(2,1)}, u32[]{:S(2)}) copy-start(bf16[1,1024,448]{1,2,0:T(8,128)(2,1)} %param.4) | copy-start | bytes 2752516
  84.2 3.6 %copy-start.11 = (bf16[1024,448]{0,1:T(8,128)(2,1)}, bf16[1024,448]{0,1:T(8,128)(2,1)S(1)}, u32[]{:S(2)}) copy-start(bf16[1024,448]{0,1:T(8,128)(2,1)S(1)} %fusion.17) | copy-start | bytes 2752516
  84.2 20.3 %collective-permute-start.6 = (bf16[1024,448]{0,1:T(8,128)(2,1)S(1)}, bf16[1024,448]{0,1:T(8,128)(2,1)S(1)}, u32[]{:S(2)}, u32[]{:S(2)}) collective-permute-start(bf16[1024,448]{0,1:T(8,128)(2,1)S(1)} %fusion.17), channel_id=1, source_target_pairs={{0,8},{4,12},{1,9},{5,13},{2,10},{6,14},{3,11},{7,15},{16,24},{20,... | collective-permute-start | bytes 2752520 | tf_op jit(solution)/shard_map/ppermute | solution.py:11
  85.7 43.5 %collective-permute-start.5 = (bf16[1024,448]{0,1:T(8,128)(2,1)S(1)}, bf16[1024,448]{0,1:T(8,128)(2,1)S(1)}, u32[]{:S(2)}, u32[]{:S(2)}) collective-permute-start(bf16[1024,448]{0,1:T(8,128)(2,1)S(1)} %fusion.17), channel_id=1, source_target_pairs={{8,0},{12,4},{9,1},{13,5},{10,2},{14,6},{11,3},{15,7},{24,16},{28,... | collective-permute-start | bytes 2752520 | tf_op jit(solution)/shard_map/ppermute | solution.py:11
  104.5 0.9 copy-start.17
  129.2 0.9 copy-start.13
  132.1 2.5 %copy-start.8 = (bf16[1,448,448]{2,1,0:T(8,128)(2,1)S(1)}, bf16[1,448,448]{2,1,0:T(8,128)(2,1)}, u32[]{:S(2)}) copy-start(bf16[1,448,448]{2,1,0:T(8,128)(2,1)} %copy.17) | copy-start | bytes 1204228
  132.1 2.5 %copy-start.12 = (bf16[1024,448]{0,1:T(8,128)(2,1)S(1)}, bf16[1024,448]{0,1:T(8,128)(2,1)}, u32[]{:S(2)}) copy-start(bf16[1024,448]{0,1:T(8,128)(2,1)} %copy-done.11) | copy-start | bytes 2752516
  134.7 1.0 copy-start.1
  134.7 1.3 copy-start.14
  136.0 1.2 copy-start.6
  136.0 1.3 copy-start.10
  136.0 1.7 copy-start.18
Sparse Core Ops, SparseCore 0:
  10.1 32.9 all-gather.1
  78.7 23.4 reduce-scatter.8
  134.8 23.4 reduce-scatter.6
